TPU v7x, 256 devices: a whole 4x4x8 slice. The times are simulated.
256 devices in a mesh: dp: 16 (over x_lo, y, core), tensor: 16 (over z, x_hi).
Axes of the slice: x: 4 (x_hi: 2, x_lo: 2; x = x_hi * 2 + x_lo), y: 4, z: 8, core: 2. Of those that a mesh axis runs over, the one named last changes fastest.
Arguments:
- target_hidden: bfloat16 [512, 16384], P('dp', 'tensor'), may hold values from -64 to 64
- target_gain: bfloat16 [16384], replicated, may hold values from 0.25 to 1.75
- target_head: bfloat16 [16384, 65536], P(None, ('dp', 'tensor')), may hold values from -8 to 8
- reference_hidden: bfloat16 [512, 4096], P('dp', 'tensor'), may hold values from -64 to 64
- reference_gain: bfloat16 [4096], replicated, may hold values from 0.25 to 1.75
- reference_head: bfloat16 [4096, 65536], P(None, ('dp', 'tensor')), may hold values from -8 to 8
Outputs:
- contrast: float32 [512, 65536], P(None, ('dp', 'tensor'))
All inputs are finite; a program needn't handle non-finite values.
Results may differ from a plain program's by a relative error of at most 0.0012.
Values may be sent and summed in bfloat16 or wider, within the bound.
No kernel may reach another device: no remote copies, remote signals or barrier semaphores. Data moves between devices by JAX's collectives and lax.ppermute only.
A program may use at most 128 MiB of HBM per device.

v0:
```python
import jax
import jax.numpy as jnp
from jax import lax
from jax.sharding import PartitionSpec as P

EPS = 1e-05
LOG_TEN = 2.302585092994046


def normalize_full(piece, gain):
    values = piece.astype(jnp.float32)
    square_mean = jnp.mean(values * values, axis=1, keepdims=True)
    return (values * lax.rsqrt(square_mean + EPS) * gain.astype(jnp.float32)).astype(jnp.bfloat16)


def local(
    target_hidden, target_gain, target_head, reference_hidden, reference_gain, reference_head
):
    wide_t, wide_r = (
        lax.all_gather(target_hidden, "tensor", axis=1, tiled=True),
        lax.all_gather(reference_hidden, "tensor", axis=1, tiled=True),
    )
    logits_t = jnp.dot(
        normalize_full(lax.all_gather(wide_t, "dp", axis=0, tiled=True), target_gain),
        target_head,
        preferred_element_type=jnp.float32,
    )
    logits_r = jnp.dot(
        normalize_full(lax.all_gather(wide_r, "dp", axis=0, tiled=True), reference_gain),
        reference_head,
        preferred_element_type=jnp.float32,
    )
    local_peak_t = jnp.max(logits_t, axis=1)
    local_peak_r = jnp.max(logits_r, axis=1)
    peak_t, peak_r = lax.pmax((local_peak_t, local_peak_r), ("dp", "tensor"))
    local_total_t = jnp.sum(jnp.exp(logits_t - peak_t[:, None]), axis=1)
    local_total_r = jnp.sum(jnp.exp(logits_r - peak_r[:, None]), axis=1)
    total_t, total_r = lax.psum((local_total_t, local_total_r), ("dp", "tensor"))
    lse_t = (peak_t + jnp.log(total_t))[:, None]
    lse_r = (peak_r + jnp.log(total_r))[:, None]
    margin = jnp.minimum(0.0, logits_t - peak_t[:, None] + LOG_TEN)
    return logits_t - lse_t - 0.5 * (logits_r - lse_r) + margin


def solution(mesh):
    placed = (
        P("dp", "tensor"),
        P(),
        P(None, ("dp", "tensor")),
        P("dp", "tensor"),
        P(),
        P(None, ("dp", "tensor")),
    )
    return jax.shard_map(
        local, mesh=mesh, in_specs=placed, out_specs=P(None, ("dp", "tensor")), check_vma=False
    )
```

profile of v0, /device:TPU:1, one launch (start us, length us, event | category | flops | bytes accessed | tf_op | source)
XLA Modules:
  0.0 408.6 jit_solution(10341636960921009847)
XLA Ops:
  6.5 0.0 copy-start
  6.5 0.0 all-gather.4.cloned.1.call-start
  6.5 0.7 all-gather.4.cloned.1.call-update
  7.3 0.0 all-gather.8.cloned.1.call-start
  7.3 42.1 %all_gather.14 = bf16[32,4096]{1,0:T(8,128)(2,1)} all-gather(bf16[32,256]{1,0:T(8,128)(2,1)} %param.9), channel_id=1, replica_groups=mesh['dp'=16,'tensor'=16] {'tensor'}, dimensions={1}, use_global_device_ids=true | all-gather | bytes 278528 | tf_op jit(solution)/shard_map/all_gather | solution.py:21
  49.4 0.0 all-gather.8.cloned.1.call-update
  49.5 0.0 all-gather.6.cloned.1.call-start
  49.5 39.4 %all-gather.4.cloned.1.call-done = bf16[32,16384]{1,0:T(8,128)(2,1)} async-done(((bf16[32,1024]{1,0:T(8,128)(2,1)}), bf16[32,16384]{1,0:T(8,128)(2,1)}) %all-gather.4.cloned.1.call-update) | async-done | bytes 1048592 | tf_op jit(solution)/shard_map/all_gather | solution.py:20
  88.9 0.0 all-gather.6.cloned.1.call-update
  88.9 0.7 convert_element_type.22
  89.6 0.8 convert_element_type.19
  90.4 41.0 %all-gather.8.cloned.1.call-done = bf16[512,4096]{1,0:T(8,128)(2,1)} async-done(((bf16[32,4096]{1,0:T(8,128)(2,1)}), bf16[512,4096]{1,0:T(8,128)(2,1)}) %all-gather.8.cloned.1.call-update) | async-done | bytes 4194320 | tf_op jit(solution)/shard_map/all_gather | solution.py:29
  131.4 3.1 fusion.7
  134.5 0.0 copy-done
  134.5 3.8 fusion.14
  138.3 89.3 %all-gather.6.cloned.1.call-done = bf16[512,16384]{1,0:T(8,128)(2,1)} async-done(((bf16[32,16384]{1,0:T(8,128)(2,1)}), bf16[512,16384]{1,0:T(8,128)(2,1)}) %all-gather.6.cloned.1.call-update) | async-done | bytes 16777232 | tf_op jit(solution)/shard_map/all_gather | solution.py:24
  227.5 7.2 %fusion = f32[512]{0:T(512)S(1)} fusion(bf16[512,16384]{1,0:T(8,128)(2,1)} %all-gather.6.cloned.1.call-done), kind=kLoop, calls=%fused_computation.2 | loop fusion | flops 25165312 | bytes 16779264 | tf_op jit(solution)/shard_map/reduce_sum | solution.py:12
  234.7 13.6 %fusion.15 = (f32[512]{0:T(512)S(1)}, f32[512,256]{0,1:T(8,128)S(1)}) fusion(bf16[16384,256]{1,0:T(8,128)(2,1)} %param.8, bf16[512,16384]{1,0:T(8,128)(2,1)} %all-gather.6.cloned.1.call-done, f32[16384]{0:T(1024)S(1)} %convert_element_type.19, f32[512]{0:T(512)S(1)} %add_rsqrt_fusion.1), kind=kOutput, calls=%fused_computation.24 | convolution fusion | flops 4328652288 | bytes 25759744 | tf_op jit(solution)/shard_map/dot_general | solution.py:23
  248.4 77.0 %all-reduce.1 = (f32[512]{0:T(512)S(1)}, f32[512]{0:T(512)S(1)}) all-reduce(f32[512]{0:T(512)S(1)} %get-tuple-element.9, f32[512]{0:T(512)S(1)} %get-tuple-element.11), channel_id=1, replica_groups=mesh['dp'=16,'tensor'=16] {'dp','tensor'}, use_global_device_ids=true, to_apply=%region_7.0 | all-reduce | flops 1024 | bytes 8192 | tf_op jit(solution)/shard_map/pmax | solution.py:35
  325.4 0.2 exponential_reduce_fusion
  325.6 73.6 %all-reduce = (f32[512]{0:T(512)S(1)}, f32[512]{0:T(512)S(1)}) all-reduce(f32[512]{0:T(512)S(1)} %get-tuple-element.13, f32[512]{0:T(512)S(1)} %get-tuple-element.14), channel_id=1, replica_groups=mesh['dp'=16,'tensor'=16] {'dp','tensor'}, use_global_device_ids=true, to_apply=%region_9.0 | all-reduce | flops 1024 | bytes 8192 | tf_op jit(solution)/shard_map/psum | solution.py:38
  399.1 0.9 minimum_add_fusion
  400.1 2.0 copy.7
  (4 shorter events, 0.0 us)
Async XLA Ops:
  6.5 128.0 %copy-start = (bf16[4096,256]{1,0:T(8,128)(2,1)S(1)}, bf16[4096,256]{1,0:T(8,128)(2,1)}, u32[]{:S(2)}) copy-start(bf16[4096,256]{1,0:T(8,128)(2,1)} %param.11) | copy-start | bytes 6291460
  6.5 82.4 %all-gather.4.cloned.1.call-start = ((), (), s32[]{:S(2)}) async-start(), calls=%async_computation | async-start | bytes 1114112 | tf_op jit(solution)/shard_map/all_gather | solution.py:20
  7.3 124.1 %all-gather.8.cloned.1.call-start = ((), (), s32[]{:S(2)}) async-start(), calls=%async_computation.2 | async-start | bytes 4456448 | tf_op jit(solution)/shard_map/all_gather | solution.py:29
  49.5 178.1 %all-gather.6.cloned.1.call-start = ((), (), s32[]{:S(2)}) async-start(), calls=%async_computation.1 | async-start | bytes 17825792 | tf_op jit(solution)/shard_map/all_gather | solution.py:24
Sparse Core Ops, SparseCore 0:
  10.0 78.8 all-gather.3
  90.7 40.6 all-gather.7
  133.3 94.2 all-gather.5
where the time goes:
time: 409 us
  blocking collectives  193 us (47%)
  waiting for transfers between devices  170 us (42%)
  matrix products  17.4 us (4%)
  between operations  13.1 us (3%)
  other arithmetic  12.9 us (3%)
    all_gather x1, waiting for transfers between devices, local(): lax.all_gather(wide_t, 'dp', axis=0, tiled=True)  89.3 us
    pmax x1, blocking collectives, local(): peak_t, peak_r = lax.pmax((local_peak_t, local_peak_r), ('dp', 'tensor'))  77 us
    psum x1, blocking collectives, local(): lax.psum((local_total_t, local_total_r), ('dp', 'tensor'))  73.6 us
    all_gather x1, blocking collectives, local(): lax.all_gather(reference_hidden, 'tensor', axis=1, tiled=True)  42.1 us
    all_gather x1, waiting for transfers between devices, local(): lax.all_gather(wide_r, 'dp', axis=0, tiled=True)  41 us
    all_gather x1, waiting for transfers between devices, local(): lax.all_gather(target_hidden, 'tensor', axis=1, tiled=True)  39.4 us
    dot_general x1, matrix products, local(): jnp.dot(normalize_full(lax.all_gather(wide_t, 'dp', axis=0, tiled=True),...  13.6 us
    reduce_sum x2, other arithmetic, normalize_full(): square_mean = jnp.mean(values * values, axis=1, keepdims=True)  10.3 us
  transfers between devices with their start and end apart: 3, of which 3 were waited for; matrix products, arithmetic and copies ran while one was open for 2% of the time, Pallas kernels for 0%

commit v1 on v0

--- a/solution.py
+++ b/solution.py
@@ -18,7 +18,10 @@
 ):
     wide_t, wide_r = (
         lax.all_gather(target_hidden, "tensor", axis=1, tiled=True),
-        lax.all_gather(reference_hidden, "tensor", axis=1, tiled=True),
+        jnp.concatenate(
+            lax.all_to_all(jnp.stack([reference_hidden] * lax.axis_size("tensor")), "tensor", 0, 0),
+            axis=1,
+        ),
     )
     logits_t = jnp.dot(
         normalize_full(lax.all_gather(wide_t, "dp", axis=0, tiled=True), target_gain),

time: 409 us -> 409 us (level)
  blocking collectives: 193 us -> 174 us
  waiting for transfers between devices: 170 us -> 188 us
    all_gather x1 -> x0, blocking collectives: 42.1 us -> none  [local(): lax.all_gather(reference_hidden, 'tensor', axis=1, tiled=True)]
    all_to_all x0 -> x1, blocking collectives: none -> 23.4 us  [local(): lax.all_to_all(jnp.stack([reference_hidden] * lax.axis_size('tensor')), '...]
    all_gather x1, waiting for transfers between devices: 39.4 us -> 56.7 us  [local(): lax.all_gather(target_hidden, 'tensor', axis=1, tiled=True)]
where the time goes in v1:
time: 409 us
  waiting for transfers between devices  188 us (46%)
  blocking collectives  174 us (43%)
  matrix products  17.4 us (4%)
  between operations  13.1 us (3%)
  other arithmetic  12.9 us (3%)
    all_gather x1, waiting for transfers between devices, local(): lax.all_gather(wide_t, 'dp', axis=0, tiled=True)  89.3 us
    pmax x1, blocking collectives, local(): peak_t, peak_r = lax.pmax((local_peak_t, local_peak_r), ('dp', 'tensor'))  77 us
    psum x1, blocking collectives, local(): lax.psum((local_total_t, local_total_r), ('dp', 'tensor'))  73.6 us
    all_gather x1, waiting for transfers between devices, local(): lax.all_gather(target_hidden, 'tensor', axis=1, tiled=True)  56.7 us
    all_gather x1, waiting for transfers between devices, local(): lax.all_gather(wide_r, 'dp', axis=0, tiled=True)  41 us
    all_to_all x1, blocking collectives, local(): lax.all_to_all(jnp.stack([reference_hidden] * lax.axis_size('tensor')), '...  23.4 us
    dot_general x1, matrix products, local(): jnp.dot(normalize_full(lax.all_gather(wide_t, 'dp', axis=0, tiled=True),...  13.6 us
    reduce_sum x2, other arithmetic, normalize_full(): square_mean = jnp.mean(values * values, axis=1, keepdims=True)  10.3 us
  transfers between devices with their start and end apart: 3, of which 3 were waited for; matrix products, arithmetic and copies ran while one was open for 2% of the time, Pallas kernels for 0%

profile of v1, /device:TPU:1, one launch (start us, length us, event | category | flops | bytes accessed | tf_op | source)
XLA Modules:
  0.0 408.7 jit_solution(14501623712414318337)
XLA Ops:
  6.5 0.0 copy-start
  6.5 0.0 all-gather.4.cloned.1.call-start
  6.5 0.7 all-gather.4.cloned.1.call-update
  7.3 0.0 all-gather.8.cloned.1.call-start
  7.3 0.7 stack.2
  8.0 23.4 %all_to_all.5 = bf16[16,32,256]{2,1,0:T(8,128)(2,1)S(1)} all-to-all(bf16[16,32,256]{2,1,0:T(8,128)(2,1)S(1)} %stack.2), channel_id=1, replica_groups=mesh['dp'=16,'tensor'=16] {'tensor'}, dimensions={0} | all-to-all | bytes 524288 | tf_op jit(solution)/shard_map/all_to_all | solution.py:22
  31.4 0.7 copy.11
  32.1 0.0 all-gather.8.cloned.1.call-update
  32.2 0.0 all-gather.6.cloned.1.call-start
  32.2 56.7 %all-gather.4.cloned.1.call-done = bf16[32,16384]{1,0:T(8,128)(2,1)} async-done(((bf16[32,1024]{1,0:T(8,128)(2,1)}), bf16[32,16384]{1,0:T(8,128)(2,1)}) %all-gather.4.cloned.1.call-update) | async-done | bytes 1048592 | tf_op jit(solution)/shard_map/all_gather | solution.py:20
  88.9 0.0 all-gather.6.cloned.1.call-update
  88.9 0.7 convert_element_type.22
  89.6 0.8 convert_element_type.19
  90.4 41.0 %all-gather.8.cloned.1.call-done = bf16[512,4096]{1,0:T(8,128)(2,1)} async-done(((bf16[32,4096]{1,0:T(8,128)(2,1)}), bf16[512,4096]{1,0:T(8,128)(2,1)}) %all-gather.8.cloned.1.call-update) | async-done | bytes 4194320 | tf_op jit(solution)/shard_map/all_gather | solution.py:32
  131.4 3.1 fusion.7
  134.5 0.0 copy-done
  134.5 3.8 fusion.14
  138.3 89.3 %all-gather.6.cloned.1.call-done = bf16[512,16384]{1,0:T(8,128)(2,1)} async-done(((bf16[32,16384]{1,0:T(8,128)(2,1)}), bf16[512,16384]{1,0:T(8,128)(2,1)}) %all-gather.6.cloned.1.call-update) | async-done | bytes 16777232 | tf_op jit(solution)/shard_map/all_gather | solution.py:27
  227.5 7.2 %fusion = f32[512]{0:T(512)S(1)} fusion(bf16[512,16384]{1,0:T(8,128)(2,1)} %all-gather.6.cloned.1.call-done), kind=kLoop, calls=%fused_computation.2 | loop fusion | flops 25165312 | bytes 16779264 | tf_op jit(solution)/shard_map/reduce_sum | solution.py:12
  234.8 13.6 %fusion.15 = (f32[512]{0:T(512)S(1)}, f32[512,256]{0,1:T(8,128)S(1)}) fusion(bf16[16384,256]{1,0:T(8,128)(2,1)} %param.8, bf16[512,16384]{1,0:T(8,128)(2,1)} %all-gather.6.cloned.1.call-done, f32[16384]{0:T(1024)S(1)} %convert_element_type.19, f32[512]{0:T(512)S(1)} %add_rsqrt_fusion.1), kind=kOutput, calls=%fused_computation.24 | convolution fusion | flops 4328652288 | bytes 25759744 | tf_op jit(solution)/shard_map/dot_general | solution.py:26
  248.4 77.0 %all-reduce.1 = (f32[512]{0:T(512)S(1)}, f32[512]{0:T(512)S(1)}) all-reduce(f32[512]{0:T(512)S(1)} %get-tuple-element.9, f32[512]{0:T(512)S(1)} %get-tuple-element.11), channel_id=1, replica_groups=mesh['dp'=16,'tensor'=16] {'dp','tensor'}, use_global_device_ids=true, to_apply=%region_7.0 | all-reduce | flops 1024 | bytes 8192 | tf_op jit(solution)/shard_map/pmax | solution.py:38
  325.4 0.2 exponential_reduce_fusion
  325.6 73.6 %all-reduce = (f32[512]{0:T(512)S(1)}, f32[512]{0:T(512)S(1)}) all-reduce(f32[512]{0:T(512)S(1)} %get-tuple-element.13, f32[512]{0:T(512)S(1)} %get-tuple-element.14), channel_id=1, replica_groups=mesh['dp'=16,'tensor'=16] {'dp','tensor'}, use_global_device_ids=true, to_apply=%region_9.0 | all-reduce | flops 1024 | bytes 8192 | tf_op jit(solution)/shard_map/psum | solution.py:41
  399.2 0.9 minimum_add_fusion
  400.1 2.0 copy.10
  (4 shorter events, 0.0 us)
Async XLA Ops:
  6.5 128.0 %copy-start = (bf16[4096,256]{1,0:T(8,128)(2,1)S(1)}, bf16[4096,256]{1,0:T(8,128)(2,1)}, u32[]{:S(2)}) copy-start(bf16[4096,256]{1,0:T(8,128)(2,1)} %param.11) | copy-start | bytes 6291460
  6.5 82.4 %all-gather.4.cloned.1.call-start = ((), (), s32[]{:S(2)}) async-start(), calls=%async_computation.1 | async-start | bytes 1114112 | tf_op jit(solution)/shard_map/all_gather | solution.py:20
  7.3 124.1 %all-gather.8.cloned.1.call-start = ((), (), s32[]{:S(2)}) async-start(), calls=%async_computation.3 | async-start | bytes 4456448 | tf_op jit(solution)/shard_map/all_gather | solution.py:32
  32.2 195.4 %all-gather.6.cloned.1.call-start = ((), (), s32[]{:S(2)}) async-start(), calls=%async_computation.2 | async-start | bytes 17825792 | tf_op jit(solution)/shard_map/all_gather | solution.py:27
Sparse Core Ops, SparseCore 0:
  10.0 78.9 all-gather.3
  90.8 40.6 all-gather.7
  133.3 94.2 all-gather.5
